TPU v7x, 32 devices: a whole 2x2x4 slice. The times are simulated.
32 devices in a mesh: group: 2 (over x), src: 4 (over z), tile: 4 (over y, core).
Axes of the slice: x: 2, y: 2, z: 4, core: 2. Of those that a mesh axis runs over, the one named last changes fastest.
Arguments:
- mask_param: float32 [2048, 256], P(('group', 'tile')), parts along dimension 0, may hold values from -6 to 6
- target_image: float32 [2048, 256], P(('group', 'tile')), parts along dimension 0, may hold values from 0 to 1
- source_weights: float32 [128], P(('group', 'src')), parts along dimension 0, may hold values from 0.36 to 8.2
- source_shifts: int32 [64, 2], P('src'), may hold values from -16 to 16, as said below
- pupil_map: float32 [2, 32, 32], replicated, may hold values from -1.4 to 1.4, as said below
Outputs:
- mask_final: float32 [2048, 256], P(('group', 'tile')), parts along dimension 0
- weights_final: float32 [128], P(('group', 'src')), parts along dimension 0
There are 2 independent parts, one for each index of `group`. A program takes and returns all parts, laid end to end along the dimension named above; an argument that names none is the same for every part. Nothing has to cross between parts.
Inputs may be any that keep to these rules, and one draw needn't show every extreme that they name: `source_shifts`: each of the two columns takes the value 16 on some source and the value -16 on another. `pupil_map`: zero outside the disc of radius 32 // 2 - 1 around box index (16, 16).
All inputs are finite; a program needn't handle non-finite values.
Results may differ from a plain program's by a relative error of at most 0.0003.
Values sent between devices are 32-bit elements; how exact they have to be, the bound alone decides.
No kernel may reach another device: no remote copies, remote signals or barrier semaphores. Data moves between devices by JAX's collectives and lax.ppermute only.
A program may use at most 64 MiB of HBM per device.

v0:
```python
import functools
import math

import jax
import jax.numpy as jnp
import ml_dtypes
import numpy as np
from jax import lax
from jax.experimental import pallas as pl
from jax.experimental.pallas import tpu as pltpu
from jax.sharding import PartitionSpec as P


MARGIN = 64
MAX_SHIFT = 16
MASK_RATE = 0.5
WEIGHT_RATE = 0.3
TINY_EPS = 1e-06
CHUNK = 32
GROUP = 2


bf16 = jnp.bfloat16
f32 = jnp.float32


def np_split(table):
    table = np.asarray(table, np.float64)
    high = table.astype(np.float32).astype(ml_dtypes.bfloat16)
    low = (table - high.astype(np.float64)).astype(np.float32).astype(ml_dtypes.bfloat16)
    return high, low


def phases(freqs, pixels, period):
    return 2.0 * math.pi * np.mod(np.outer(freqs, pixels), period) / period


def make_tables(tile_len, box_len, max_shift):
    period = tile_len + 2 * MARGIN
    grid = box_len + 2 * max_shift
    wide = np.arange(grid) - grid // 2
    pix = np.arange(tile_len)
    full = np.arange(period)
    points = np.arange(grid)
    box = np.arange(box_len)
    out = {}
    ang = phases(wide, pix, period)
    high, low = np_split(np.concatenate([np.cos(ang), -np.sin(ang)], 0).T / (period * tile_len))
    out["spec_cols"] = np.concatenate([high, low], 1)
    ang_rows = phases(wide, full, period)
    high, low = np_split(np.concatenate([np.cos(ang_rows), np.sin(ang_rows)], 0))
    out["spec_rows"] = np.concatenate([high, low], 0)
    ang = phases(points, points, grid)
    cos, sin = np.cos(ang), np.sin(ang)
    for name, table in (
        ("lane_fwd", np.block([[cos, sin], [-sin, cos]])),
        ("lane_back", np.block([[cos, -sin], [sin, cos]])),
    ):
        high, low = np_split(table)
        out[name] = np.block([[high, low], [high, np.zeros_like(low)]])
    ang = phases(points, box, grid)
    high, low = np_split(np.concatenate([np.cos(ang), np.sin(ang)], 1))
    out["row_fwd"] = np.concatenate([high, high, low], 1)
    high, low = np_split(np.concatenate([np.cos(ang).T, np.sin(ang).T], 0))
    out["row_back"] = np.concatenate([high, high, low], 1)

    def dirichlet(offset):
        theta = 2.0 * math.pi * ((pix + offset)[None, :] / period - points[:, None] / grid)
        orders = np.arange(1, box_len)
        return 1.0 + 2.0 * np.cos(orders[:, None, None] * theta[None]).sum(0)

    rows, cols = dirichlet(MARGIN), dirichlet(0)
    high, low = np_split(rows @ rows.T / grid)
    out["mix_rows"] = np.concatenate([high, high, low], 1)
    mix = cols @ cols.T / grid
    high, low = np_split(np.block([[mix, mix], [mix, mix]]))
    out["mix_cols"] = np.block([[high, low], [high, np.zeros_like(low)]])
    high, low = np_split(rows)
    out["target_rows"] = np.concatenate([high, low], 0)
    high, low = np_split(np.concatenate([cols, cols], 0).T)
    out["target_cols"] = np.concatenate([high, low], 1)
    ang = phases(wide, pix, period)
    cos, sin = np.cos(ang), np.sin(ang)
    high, low = np_split(np.block([[cos, -sin], [-sin, -cos]]))
    out["grad_cols"] = np.concatenate([high, high, low], 0)
    ang = phases(full, np.arange(grid // 2), period)
    high, low = np_split(np.concatenate([np.cos(ang), np.sin(ang)], 1))
    out["grad_rows"] = np.concatenate([high, high, low], 1)
    return out


def pack_tables(tables):
    wide = [n for n in tables if tables[n].shape[1] > 256]
    narrow = sorted((n for n in tables if n not in wide), key=lambda n: -tables[n].shape[0])
    place, heights = {}, [0, 0]
    for n in wide:
        place[n] = (heights[0], 0)
        heights = [heights[0] + tables[n].shape[0]] * 2
    for n in narrow:
        side = int(heights[1] < heights[0])
        place[n] = (heights[side], 256 * side)
        heights[side] += tables[n].shape[0]
    whole = np.zeros((max(heights), 512), ml_dtypes.bfloat16)
    spots = {}
    for n, (row, col) in place.items():
        rows, cols = tables[n].shape
        whole[row : row + rows, col : col + cols] = tables[n]
        spots[n] = (slice(row, row + rows), slice(col, col + cols))
    return whole, spots


def split(value):
    high = value.astype(bf16)
    return high, (value - high.astype(f32)).astype(bf16)


def dot(left, right):
    return jnp.dot(left, right, preferred_element_type=f32)


def halves(value):
    width = value.shape[1] // 2
    return value[:, :width] + value[:, width:]


def lane_sign(rows, lanes, first):
    lane = lax.broadcasted_iota(jnp.int32, (rows, lanes), 1)
    return jnp.where(lane < lanes // 2, first, -first).astype(f32)


def swap(value):
    return pltpu.roll(value, value.shape[1] // 2, 1)


def half_tanh(value):
    return jnp.tanh(0.5 * value)


def sigmoid(value):
    return 0.5 * half_tanh(value) + 0.5


def window_spectrum(window, t):
    grid = t["spec_cols"].shape[1] // 4
    high, low = split(window)
    cols = t["spec_cols"]
    mid = halves(dot(high, cols[...])) + dot(low, cols[:, : 2 * grid])
    mid_high, mid_low = split(mid)
    rows = t["spec_rows"]
    both = halves(dot(rows[: 2 * grid, :], jnp.concatenate([mid_high, mid_low], 1)))
    both = both + dot(rows[2 * grid :, :], mid_high)
    return both[:grid] + lane_sign(grid, 2 * grid, 1.0) * swap(both[grid:])


def skewed(count, stages, first, second, carry):
    chunks = count // CHUNK
    first(0, stages[0])
    for c in range(1, chunks):
        first(c, stages[c % 2])
        carry = second(c - 1, stages[(c - 1) % 2], carry)
    return second(chunks - 1, stages[(chunks - 1) % 2], carry)


def turn_pupils(pupil, turned_re, turned_im):
    count, size, lanes = turned_re.shape
    grid = lanes // 2
    turned_re[0] = jnp.zeros((size, lanes), f32)
    turned_im[0] = jnp.zeros((size, lanes), f32)
    turned_re[0, :, :size] = pupil[0]
    turned_re[0, :, grid : grid + size] = pupil[0]
    turned_im[0, :, :size] = -pupil[1]
    turned_im[0, :, grid : grid + size] = pupil[1]
    real, imag = turned_re[0], turned_im[0]
    for by in range(1, count):
        turned_re[by] = pltpu.roll(real, by, 1)
        turned_im[by] = pltpu.roll(imag, by, 1)


def placed_pupils(shifts, roots, turned_re, turned_im, pr, pi):
    def make(s):
        by = shifts[2, s] + MAX_SHIFT
        real, imag = turned_re[by] * roots[3, s], turned_im[by] * roots[3, s]
        pr[s], pi[s] = real, imag
        return real, imag

    return make


def grid_fields(spec, shifts, t, pupils, work, squares=False):
    plain, crossed, fields, *stages = work
    count, grid, lanes = fields.shape
    box_len = t["row_fwd"].shape[1] // 6
    plain[...] = spec
    crossed[...] = swap(spec)
    sign = lane_sign(box_len, lanes, -1.0)

    def first(c, stage):
        rows = []
        for i in range(CHUNK):
            s = c * CHUNK + i
            at = pl.ds(shifts[1, s] + MAX_SHIFT, box_len)
            real, imag = pupils(s)
            high, low = split(real * plain[at, :] + imag * crossed[at, :])
            rows.append(jnp.concatenate([high, low], 1))
        stage[...] = halves(dot(jnp.concatenate(rows, 0), t["lane_fwd"][...]))

    def second(c, stage, power):
        for base in range(0, CHUNK, GROUP):
            stacks = []
            for i in range(base, base + GROUP):
                part = stage[i * box_len : (i + 1) * box_len, :]
                high, low = split(jnp.concatenate([part, sign * swap(part)], 0))
                stacks.append(jnp.concatenate([high, low, high], 0))
            out = dot(t["row_fwd"][...], jnp.concatenate(stacks, 1))
            for i in range(GROUP):
                field = out[:, i * lanes : (i + 1) * lanes]
                square = field * field
                fields[c * CHUNK + base + i] = square if squares else field
                power = power + square
        return power

    return skewed(count, stages, first, second, jnp.zeros((grid, lanes), f32))


def grid_misfit(power, inv_dose, target, t):
    high, low = split(power)
    mid = halves(dot(jnp.concatenate([high, low], 1), t["mix_cols"][...]))
    high, low = split(mid)
    lit = dot(t["mix_rows"][...], jnp.concatenate([high, low, high], 0))
    return lit * inv_dose - target


def gather_back(misfit, shifts, scale, t, pr, pi, fields, stages, sums):
    count, box_len, lanes = pr.shape
    grid = lanes // 2
    for ref in sums:
        ref[...] = jnp.zeros_like(ref)
    sign = lane_sign(box_len, lanes, 1.0)

    def first(c, stage):
        for base in range(0, CHUNK, GROUP):
            stacks = []
            for i in range(base, base + GROUP):
                high, low = split(fields[c * CHUNK + i] * misfit)
                stacks.append(jnp.concatenate([high, low, high], 0))
            both = dot(t["row_back"][...], jnp.concatenate(stacks, 1))
            for i in range(GROUP):
                part = both[:, i * lanes : (i + 1) * lanes]
                at = (base + i) * box_len
                stage[at : at + box_len, :] = part[:box_len] + sign * swap(part[box_len:])

    def second(c, stage, carry):
        high, low = split(stage[...])
        hits = halves(dot(jnp.concatenate([high, low], 1), t["lane_back"][...]))
        for i in range(CHUNK):
            s = c * CHUNK + i
            rows = pl.ds(shifts[1, s] + MAX_SHIFT, box_len)
            hit = hits[i * box_len : (i + 1) * box_len]
            one, two = sums[2 * (i % 2)], sums[2 * (i % 2) + 1]
            one[rows, :] += pr[s] * hit
            two[rows, :] += pi[s] * hit
        return carry

    skewed(count, stages, first, second, 0)
    whole, turned = sums[0], sums[1]
    whole[...] = (whole[...] + sums[2][...] + swap(turned[...] + sums[3][...])) * scale
    middle = grid // 2
    turned[0:1, :] = jnp.zeros((1, lanes), f32)
    for a in range(1, middle):
        turned[a : a + 1, :] = whole[middle - a : middle - a + 1, :]
    ahead, behind = whole[middle:, :], turned[:middle, :]
    return jnp.concatenate([ahead + behind, ahead - behind], 0)


def tile_of(k, tile):
    return lax.bitwise_xor(tile, jnp.int32(k))


def fill_windows(backs, t, tile, tiles, wins):
    half = backs[0].shape[0] // 2
    tile_len = wins.shape[2]
    stacks = []
    for rows in (slice(0, half), slice(half, 2 * half)):
        parts = []
        for back in backs:
            high, low = split(back[rows, :])
            parts.append(jnp.concatenate([high, low, high], 1))
        stacks.append(jnp.concatenate(parts, 0))
    even = dot(stacks[0], t["grad_cols"][:, :tile_len])
    odd = dot(stacks[1], t["grad_cols"][:, tile_len:])
    wins[0, MARGIN + tile_len :, :] = jnp.zeros((MARGIN, tile_len), f32)
    wins[tiles + 1, :MARGIN, :] = jnp.zeros((MARGIN, tile_len), f32)
    for k in range(tiles):
        at = slice(k * half, (k + 1) * half)
        high, low = split(jnp.concatenate([even[at], odd[at]], 0))
        out = dot(t["grad_rows"][...], jnp.concatenate([high, low, high], 0))
        wins[tile_of(k, tile) + 1] = out


def pieces(tile_len):
    return (
        (0, MARGIN, 0, tile_len),
        (MARGIN, tile_len - MARGIN, 1, 0),
        (tile_len - MARGIN, tile_len, 2, -tile_len),
    )


def piece_total(own, piece, wins):
    low, high, near, shift = piece
    total = wins[own + 1, MARGIN + low : MARGIN + high, :]
    if near != 1:
        at = MARGIN + low + shift
        total = total + wins[own + near, at : at + MARGIN, :]
    return total


def squares_of(grad):
    return jnp.sum((grad * grad).reshape(-1, 8, grad.shape[1]), axis=0)


def step_rate(square, tiles):
    tile_len = square.shape[1]
    total = jnp.sum(jnp.sum(square, axis=0, keepdims=True), axis=1, keepdims=True)
    return MASK_RATE / jnp.sqrt(total / (tiles * tile_len * tile_len) + TINY_EPS)


def slope_of(params):
    lean = half_tanh(params)
    return 1.0 - lean * lean


def near_tiles(tile, tiles):
    prev, follow = jnp.maximum(tile - 1, 0), jnp.minimum(tile + 1, tiles - 1)
    return prev, follow, (tile > 0).astype(f32), (tile < tiles - 1).astype(f32)


def edge_params(tile, mate, cross):
    odd = lax.rem(tile, 2) > 0
    before = jnp.where(odd, mate[-MARGIN:, :], cross[...])
    after = jnp.where(odd, cross[...], mate[:MARGIN, :])
    return before, after


def mask_window(near, has_prev, has_next):
    rows = near.shape[0]
    return jnp.concatenate(
        [
            sigmoid(near[:MARGIN, :]) * has_prev,
            sigmoid(near[MARGIN : rows - MARGIN, :]),
            sigmoid(near[rows - MARGIN :, :]) * has_next,
        ],
        0,
    )


def start_all(pairs, sems):
    copies = [pltpu.make_async_copy(a, b, sems.at[i]) for i, (a, b) in enumerate(pairs)]
    for copy in copies:
        copy.start()
    return copies


def head_kernel(out):
    out[...] = jnp.zeros_like(out)


def mark_kernel(value, out):
    out[...] = value[...]


def pack_kernel(place, head, weights, shifts, packed):
    local = weights.shape[1]
    packed[...] = head[...]
    packed[0:1, :local] = weights[...]
    packed[1:3, :local] = shifts[...].astype(f32)
    packed[3:4, :local] = jnp.sqrt(weights[...])
    packed[...] = pltpu.roll(packed[...], place[0] * local, 1)


def edge_kernel(tile, mask, edge):
    at = pl.multiple_of(lax.rem(tile[0], 2) * (mask.shape[0] - MARGIN), MARGIN)
    edge[...] = mask[pl.ds(at, MARGIN), :]


def target_terms(target, t):
    rows, cols = t["target_rows"], t["target_cols"]
    grid = rows.shape[0] // 2
    high, low = split(target)
    both = dot(rows[...], high)
    mid = both[:grid] + both[grid:] + dot(rows[:grid, :], low)
    high, low = split(mid)
    return halves(dot(high, cols[...])) + dot(low, cols[:, : 2 * grid])


def doses(info, scale):
    dose = jnp.sum(info[0:1, :], axis=1, keepdims=True)
    return 1.0 / dose, scale / dose


def early_kernel(spots, table, pupil, goal, own, mate, target, turned_re, turned_im, slopes):
    t = {n: table.at[spot] for n, spot in spots.items()}
    turn_pupils(pupil, turned_re, turned_im)
    target[...] = target_terms(goal[...], t)
    slopes[0] = slope_of(own[...])
    slopes[1] = slope_of(mate[...])


def first_kernel(spots, peers, tiles, scale, tile, table, own, mate, cross,
                 target, turned_re, turned_im, *refs):
    parts = refs[:peers]
    t = {n: table.at[spot] for n, spot in spots.items()}
    back, pr, pi, info, whole, near = refs[peers : peers + 6]
    *work, s0, s1, s2, s3, shifts, roots, sems = refs[peers + 6 :]
    total = parts[0][...]
    for part in parts[1:]:
        total = total + part[...]
    info[...] = total
    whole[...] = total.astype(jnp.int32)
    copies = start_all(((whole, shifts), (info, roots)), sems)
    here = tile[0]
    tile_len = own.shape[0]
    _, _, has_prev, has_next = near_tiles(here, tiles)
    before, after = edge_params(here, mate, cross)
    near[:MARGIN, :] = before
    near[MARGIN : MARGIN + tile_len, :] = own[...]
    near[MARGIN + tile_len :, :] = after
    spec = window_spectrum(mask_window(near, has_prev, has_next), t)
    for copy in copies:
        copy.wait()
    pupils = placed_pupils(shifts, roots, turned_re, turned_im, pr, pi)
    power = grid_fields(spec, shifts, t, pupils, work)
    inv_dose, factor = doses(total, scale)
    misfit = grid_misfit(power, inv_dose, target[...], t)
    sums = (s0, s1, s2, s3)
    back[...] = gather_back(misfit, shifts, factor, t, pr, pi, work[2], work[3:], sums)


def next_kernel(spots, tiles, scale, tile, table, shifts, info, pr, pi, target, near, slopes, *refs):
    params, backs = refs[: tiles - 2], refs[tiles - 2 : 2 * tiles - 2]
    t = {n: table.at[spot] for n, spot in spots.items()}
    new, grads, rates, back, *work, s0, s1, s2, s3, wins = refs[2 * tiles - 2 :]
    here = tile[0]
    tile_len = wins.shape[2]
    fill_windows(backs, t, here, tiles, wins)
    square = jnp.zeros((8, tile_len), f32)
    for k in range(tiles):
        own = tile_of(k, here)
        for piece in pieces(tile_len):
            low, high = piece[:2]
            slope = slopes[k, low:high, :] if k < 2 else slope_of(params[k - 2][low:high, :])
            grad = piece_total(own, piece, wins) * slope
            grads[own, low:high, :] = grad
            square = square + squares_of(grad)
    rate = step_rate(square, tiles)
    rates[...] = jnp.broadcast_to(rate, rates.shape)
    prev, follow, has_prev, has_next = near_tiles(here, tiles)
    inner = slice(MARGIN, MARGIN + tile_len)
    new[:MARGIN, :] = near[:MARGIN, :] - grads[prev, tile_len - MARGIN :, :] * rate
    new[inner, :] = near[inner, :] - grads[here] * rate
    new[MARGIN + tile_len :, :] = near[MARGIN + tile_len :, :] - grads[follow, :MARGIN, :] * rate
    spec = window_spectrum(mask_window(new, has_prev, has_next), t)
    power = grid_fields(spec, shifts, t, lambda s: (pr[s], pi[s]), work)
    inv_dose, factor = doses(info[...], scale)
    misfit = grid_misfit(power, inv_dose, target[...], t)
    sums = (s0, s1, s2, s3)
    back[...] = gather_back(misfit, shifts, factor, t, pr, pi, work[2], work[3:], sums)


def slope_kernel(tiles, tile, grads, rates, *refs):
    params, slopes = refs[:tiles], refs[tiles]
    rate = rates[0:1, 0:1]
    for k in range(tiles):
        own = tile_of(k, tile[0])
        slopes[own] = slope_of(params[k][...] - grads[own] * rate)


def last_kernel(spots, tiles, tile, table, shifts, info, pr, pi, target, near, slopes, *refs):
    backs = refs[:tiles]
    t = {n: table.at[spot] for n, spot in spots.items()}
    final, row, *work, terms, wins, fresh, sems = refs[tiles:]
    fields = work[2]
    here = tile[0]
    tile_len = wins.shape[2]
    fill_windows(backs, t, here, tiles, wins)

    def grad_of(own, piece):
        return piece_total(own, piece, wins) * slopes[own, piece[0] : piece[1], :]

    square = jnp.zeros((8, tile_len), f32)
    for own in range(tiles):
        for piece in pieces(tile_len):
            square = square + squares_of(grad_of(own, piece))
    rate = step_rate(square, tiles)
    prev, follow, has_prev, has_next = near_tiles(here, tiles)
    first, *_, end = pieces(tile_len)
    fresh[:MARGIN, :] = near[:MARGIN, :] - grad_of(prev, end) * rate
    for piece in pieces(tile_len):
        at = slice(MARGIN + piece[0], MARGIN + piece[1])
        fresh[at, :] = near[at, :] - grad_of(here, piece) * rate
    fresh[MARGIN + tile_len :, :] = near[MARGIN + tile_len :, :] - grad_of(follow, first) * rate
    (leave,) = start_all(((fresh.at[pl.ds(MARGIN, tile_len), :], final),), sems)
    spec = window_spectrum(mask_window(fresh, has_prev, has_next), t)
    power = grid_fields(
        spec, shifts, t, lambda s: (pr[s], pi[s]), work, squares=True
    )
    inv_dose, _ = doses(info[...], 1.0)
    misfit = grid_misfit(power, inv_dose, target[...], t)

    def chunk(c, carry):
        rows = []
        for i in range(CHUNK):
            rows.append(jnp.sum(fields[c * CHUNK + i] * misfit, axis=0, keepdims=True))
        terms[pl.ds(pl.multiple_of(c * CHUNK, CHUNK), CHUNK), :] = jnp.concatenate(rows, 0)
        return carry

    count = fields.shape[0]
    lax.fori_loop(0, count // CHUNK, chunk, 0)
    high, low = split(terms[...])
    left = terms[...] - high.astype(f32) - low.astype(f32)
    ones = jnp.ones((8, terms.shape[1]), bf16)
    total = jnp.zeros((8, terms.shape[0]), f32)
    for part in (left.astype(bf16), low, high):
        total = total + lax.dot_general(
            ones, part, (((1,), (1,)), ((), ())), preferred_element_type=f32
        )
    row[...] = total
    leave.wait()


def weight_kernel(tiles, scale, tile, place, info, *refs):
    rows = refs[:tiles]
    out, stack = refs[tiles:]
    count = rows[0].shape[1]
    for k in range(tiles):
        stack[k] = rows[k][...]
    here = tile[0]
    total = stack[here]
    for k in range(1, tiles):
        total = total + stack[tile_of(k, here)]
    summed = total[0:1] * scale
    weight = info[0:1, :count]
    dose = jnp.sum(weight, axis=1, keepdims=True)
    mean = jnp.sum(summed, axis=1, keepdims=True) / dose
    grad = (summed / weight - mean) / dose
    spread = jnp.sqrt(jnp.sum(grad * grad, axis=1, keepdims=True) / count + TINY_EPS)
    new = weight * jnp.exp(-WEIGHT_RATE * grad / spread)
    size = out.shape[1]
    lanes = info.shape[1]
    if count < lanes:
        new = jnp.concatenate([new, jnp.zeros((1, lanes - count), f32)], 1)
    new = pltpu.roll(jnp.broadcast_to(new, (8, lanes)), lanes - place[0] * size, 1)
    out[...] = new[0:1, :size]


def crossed(value, axis, k):
    return lax.ppermute(value, axis, [(i, i ^ k) for i in range(lax.axis_size(axis))])


def all_of(value, axis):
    got = [value]
    for k in range(1, lax.axis_size(axis)):
        got.append(crossed(value, axis, k))
    return got


def per_device(mask_param, target_image, source_weights, source_shifts, pupil_map):
    tile_len = mask_param.shape[1]
    box_len = pupil_map.shape[1]
    grid = box_len + 2 * MAX_SHIFT
    lanes = 2 * grid
    tiles = lax.axis_size("tile")
    peers = lax.axis_size("src")
    local = source_weights.shape[0]
    count = local * peers
    assert tiles & (tiles - 1) == 0 and peers & (peers - 1) == 0 and count <= 128 and count % CHUNK == 0
    tables = make_tables(tile_len, box_len, MAX_SHIFT)

    tile = lax.axis_index("tile").astype(jnp.int32).reshape(1)
    place = lax.axis_index("src").astype(jnp.int32).reshape(1)

    vmem = pl.BlockSpec(memory_space=pltpu.VMEM)
    smem = pl.BlockSpec(memory_space=pltpu.SMEM)
    left = pl.BlockSpec(memory_space=pltpu.HBM)
    params_of = pltpu.CompilerParams(vmem_limit_bytes=32 << 20)

    def struct(*shape, kind=f32):
        return jax.ShapeDtypeStruct(shape, kind)

    def cost(flops):
        return pl.CostEstimate(flops=flops, bytes_accessed=1 << 20, transcendentals=0)

    head = pl.pallas_call(
        head_kernel,
        out_shape=struct(8, 128),
        out_specs=vmem,
        compiler_params=params_of,
        cost_estimate=cost(1 << 34),
        name="head_step",
    )()
    packed = pl.pallas_call(
        pack_kernel,
        out_shape=struct(8, 128),
        in_specs=[smem] + [vmem] * 3,
        out_specs=vmem,
        compiler_params=params_of,
        cost_estimate=cost(1 << 20),
        name="pack_sources",
    )(place, head, source_weights[None], source_shifts.T)
    _, mask_now = lax.optimization_barrier((packed, mask_param))
    edge = pl.pallas_call(
        edge_kernel,
        out_shape=struct(MARGIN, tile_len),
        in_specs=[smem, vmem],
        out_specs=vmem,
        compiler_params=params_of,
        cost_estimate=cost(1 << 20),
        name="edge_rows",
    )(tile, mask_now)
    packed = all_of(packed, "src")

    pairs = [(i, (i + 1) % tiles) for i in range(1, tiles, 2)]
    cross = lax.ppermute(edge, "tile", pairs + [(j, i) for i, j in pairs])
    mate = crossed(mask_param, "tile", 1)
    far = [crossed(mask_param, "tile", k) for k in range(2, tiles, 2)]

    whole, spots = pack_tables(tables)
    table = jnp.asarray(whole)
    work = [
        pltpu.VMEM((grid, lanes), f32),
        pltpu.VMEM((grid, lanes), f32),
        pltpu.VMEM((count, grid, lanes), f32),
        pltpu.VMEM((CHUNK * box_len, lanes), f32),
        pltpu.VMEM((CHUNK * box_len, lanes), f32),
    ]
    hold = [pltpu.VMEM((grid, lanes), f32)] * 4
    period = tile_len + 2 * MARGIN
    steps = [pltpu.VMEM((tiles + 2, period, tile_len), f32)]
    scale = 0.5 / (grid * grid * period * tile_len)
    source_len = struct(count, box_len, lanes)

    target, *turned, slopes = pl.pallas_call(
        functools.partial(early_kernel, spots),
        out_shape=[struct(grid, lanes)]
        + [struct(2 * MAX_SHIFT + 1, box_len, lanes)] * 2
        + [struct(2, tile_len, tile_len)],
        in_specs=[vmem] * 5,
        out_specs=[vmem] * 4,
        compiler_params=params_of,
        cost_estimate=cost(1 << 30),
        name="early_step",
    )(table, pupil_map, target_image, mask_param, mate)

    back, pr, pi, info, whole, near = pl.pallas_call(
        functools.partial(first_kernel, spots, peers, tiles, scale),
        out_shape=[struct(grid, lanes), source_len, source_len, struct(8, 128),
                   struct(8, 128, kind=jnp.int32), struct(period, tile_len)],
        in_specs=[smem] + [vmem] * (7 + peers),
        out_specs=[vmem] * 6,
        scratch_shapes=work + hold + [
            pltpu.SMEM((8, 128), jnp.int32),
            pltpu.SMEM((8, 128), f32),
            pltpu.SemaphoreType.DMA((2,)),
        ],
        compiler_params=params_of,
        cost_estimate=cost(1 << 32),
        name="first_step",
    )(tile, table, mask_param, mate, cross, target, *turned, *packed)

    shared = (tile, table, whole, info, pr, pi, target)
    shared_specs = [smem, vmem, smem] + [vmem] * 4

    backs = all_of(back, "tile")
    backs[0] = pl.pallas_call(
        mark_kernel,
        out_shape=struct(grid, lanes),
        in_specs=[vmem],
        out_specs=vmem,
        compiler_params=params_of,
        cost_estimate=cost(1 << 20),
        name="mark_step",
    )(back)
    far, backs[0] = lax.optimization_barrier((far, backs[0]))
    entries = [mask_param, mate]
    for one in far:
        entries += [one, crossed(one, "tile", 1)]
    near, grads, rates, back = pl.pallas_call(
        functools.partial(next_kernel, spots, tiles, scale),
        out_shape=[struct(period, tile_len), struct(tiles, tile_len, tile_len),
                   struct(8, 128), struct(grid, lanes)],
        in_specs=shared_specs + [vmem] * (2 * tiles),
        out_specs=[vmem] * 4,
        scratch_shapes=work + hold + steps,
        compiler_params=params_of,
        cost_estimate=cost(1 << 32),
        name="next_step",
    )(*shared, near, slopes, *entries[2:], *backs)

    backs = all_of(back, "tile")
    slopes = pl.pallas_call(
        functools.partial(slope_kernel, tiles),
        out_shape=struct(tiles, tile_len, tile_len),
        in_specs=[smem] + [vmem] * (2 + tiles),
        out_specs=vmem,
        compiler_params=params_of,
        cost_estimate=cost(1 << 28),
        name="slope_step",
    )(tile, grads, rates, *entries)
    final, row = pl.pallas_call(
        functools.partial(last_kernel, spots, tiles),
        out_shape=[struct(tile_len, tile_len), struct(8, count)],
        in_specs=shared_specs + [vmem] * (2 + tiles),
        out_specs=[left, vmem],
        scratch_shapes=work + [pltpu.VMEM((count, lanes), f32)] + steps + [
            pltpu.VMEM((period, tile_len), f32),
            pltpu.SemaphoreType.DMA((1,)),
        ],
        compiler_params=params_of,
        cost_estimate=cost(1 << 32),
        name="last_step",
    )(*shared, near, slopes, *backs)

    rows = all_of(row, "tile")
    out = pl.pallas_call(
        functools.partial(weight_kernel, tiles, 1.0 / (grid * grid)),
        out_shape=struct(1, local),
        in_specs=[smem] * 2 + [vmem] * (1 + tiles),
        out_specs=vmem,
        scratch_shapes=[pltpu.VMEM((tiles, 8, count), f32)],
        compiler_params=params_of,
        name="weight_step",
    )(tile, place, info, *rows)
    return final, out.reshape(local)


def solution(mesh):
    in_specs = (
        P(("group", "tile"), None),
        P(("group", "tile"), None),
        P(("group", "src")),
        P("src", None),
        P(),
    )
    out_specs = (P(("group", "tile"), None), P(("group", "src")))
    return jax.shard_map(
        per_device, mesh=mesh, in_specs=in_specs, out_specs=out_specs, check_vma=False
    )
```

profile of v0, /device:TPU:0, one launch (start us, length us, event | category | flops | bytes accessed | tf_op | source)
XLA Modules:
  0.0 43.4 jit_solution(4215922892893209325)
XLA Ops:
  0.7 0.6 %collective-permute-start = (f32[256,256]{1,0:T(8,128)}, f32[256,256]{1,0:T(8,128)S(1)}, u32[]{:S(2)}, u32[]{:S(2)}) collective-permute-start(f32[256,256]{1,0:T(8,128)} %refs_0_.1), channel_id=1, source_target_pairs={{0,1},{1,0},{2,3},{3,2},{4,5},{5,4},{6,7},{7,6},{8,9},{9,8},{10,11... | collective-permute-start | bytes 786440 | tf_op jit(solution)/shard_map/ppermute | solution.py:556
  1.6 3.1 %collective-permute-start.2 = (f32[8,128]{1,0:T(8,128)S(1)}, f32[8,128]{1,0:T(8,128)S(1)}, u32[]{:S(2)}, u32[]{:S(2)}) collective-permute-start(f32[8,128]{1,0:T(8,128)S(1)} %pack_sources.1.refs_0_), channel_id=1, source_target_pairs={{0,4},{4,0},{8,12},{12,8},{1,5},{5,1},{9,13},{13,9},{2,6},{6,2},{1... | collective-permute-start | bytes 12296 | tf_op jit(solution)/shard_map/ppermute | solution.py:556
  4.6 2.6 %collective-permute-start.3 = (f32[8,128]{1,0:T(8,128)S(1)}, f32[8,128]{1,0:T(8,128)S(1)}, u32[]{:S(2)}, u32[]{:S(2)}) collective-permute-start(f32[8,128]{1,0:T(8,128)S(1)} %pack_sources.1.refs_0_), channel_id=1, source_target_pairs={{0,8},{4,12},{8,0},{12,4},{1,9},{5,13},{9,1},{13,5},{2,10},{6,14},... | collective-permute-start | bytes 12296 | tf_op jit(solution)/shard_map/ppermute | solution.py:556
  7.2 1.7 %collective-permute-start.5 = (f32[256,256]{1,0:T(8,128)S(1)}, f32[256,256]{1,0:T(8,128)S(1)}, u32[]{:S(2)}, u32[]{:S(2)}) collective-permute-start(f32[256,256]{1,0:T(8,128)S(1)} %copy-done), channel_id=1, source_target_pairs={{0,2},{1,3},{2,0},{3,1},{4,6},{5,7},{6,4},{7,5},{8,10},{9,11},{10,... | collective-permute-start | bytes 786440 | tf_op jit(solution)/shard_map/ppermute | solution.py:556
  9.1 0.4 early_step.1
  9.5 3.1 %collective-permute-done.4.refs_3_ = f32[8,128]{1,0:T(8,128)S(1)} collective-permute-done((f32[8,128]{1,0:T(8,128)S(1)}, f32[8,128]{1,0:T(8,128)S(1)}, u32[]{:S(2)}, u32[]{:S(2)}) %collective-permute-start.4) | collective-permute-done | bytes 4128 | tf_op jit(solution)/shard_map/ppermute | solution.py:556
  12.6 2.5 %collective-permute-done.1.cross = f32[64,256]{1,0:T(8,128)S(1)} collective-permute-done((f32[64,256]{1,0:T(8,128)S(1)}, f32[64,256]{1,0:T(8,128)S(1)}, u32[]{:S(2)}, u32[]{:S(2)}) %collective-permute-start.1) | collective-permute-done | bytes 65568 | tf_op jit(solution)/shard_map/ppermute | solution.py:622
  15.1 4.1 %first_step.1 = (f32[64,128]{1,0:T(8,128)S(1)}, f32[64,32,128]{2,1,0:T(8,128)S(1)}, f32[64,32,128]{2,1,0:T(8,128)S(1)}, f32[8,128]{1,0:T(8,128)S(1)}, s32[8,128]{1,0:T(8,128)S(1)}, /*index=5*/f32[384,256]{1,0:T(8,128)S(1)}) custom-call(s32[1]{0:T(128)} %bitcast.tile, bf16[1664,512]{1,0:T(8,128)(2,1)S(1)} %copy-done.5, f32[256,256]{1,0:T(8,128)S(1)} %copy-done, ...), custom_call_target="tpu_custom_call" | custom-call | flops 4294967296 | bytes 1048576 | tf_op jit(solution)/shard_map/first_step/pallas_call | solution.py:653
  19.2 0.9 %collective-permute-start.6 = (f32[256,256]{1,0:T(8,128)S(1)}, f32[256,256]{1,0:T(8,128)S(1)}, u32[]{:S(2)}, u32[]{:S(2)}) collective-permute-start(f32[256,256]{1,0:T(8,128)S(1)} %collective-permute-done.5.refs_0_.refs_2_), channel_id=1, source_target_pairs={{0,1},{1,0},{2,3},{3,2},{4,5},{5,4},{6,7},{7,6},{8,9},{9,8},{10,11... | collective-permute-start | bytes 786440 | tf_op jit(solution)/shard_map/ppermute | solution.py:556
  20.2 1.5 %collective-permute-start.8 = (f32[64,128]{1,0:T(8,128)S(1)}, f32[64,128]{1,0:T(8,128)S(1)}, u32[]{:S(2)}, u32[]{:S(2)}) collective-permute-start(f32[64,128]{1,0:T(8,128)S(1)} %get-tuple-element.31.value), channel_id=1, source_target_pairs={{0,2},{1,3},{2,0},{3,1},{4,6},{5,7},{6,4},{7,5},{8,10},{9,11},{10,... | collective-permute-start | bytes 98312 | tf_op jit(solution)/shard_map/ppermute | solution.py:556
  22.0 2.1 %collective-permute-done.8.refs_4_ = f32[64,128]{1,0:T(8,128)S(1)} collective-permute-done((f32[64,128]{1,0:T(8,128)S(1)}, f32[64,128]{1,0:T(8,128)S(1)}, u32[]{:S(2)}, u32[]{:S(2)}) %collective-permute-start.8) | collective-permute-done | bytes 32800 | tf_op jit(solution)/shard_map/ppermute | solution.py:556
  24.1 1.0 %collective-permute-done.9.refs_5_ = f32[64,128]{1,0:T(8,128)S(1)} collective-permute-done((f32[64,128]{1,0:T(8,128)S(1)}, f32[64,128]{1,0:T(8,128)S(1)}, u32[]{:S(2)}, u32[]{:S(2)}) %collective-permute-start.9) | collective-permute-done | bytes 32800 | tf_op jit(solution)/shard_map/ppermute | solution.py:556
  25.1 5.0 %next_step.1 = (f32[384,256]{1,0:T(8,128)S(1)}, f32[4,256,256]{2,1,0:T(8,128)S(1)}, f32[8,128]{1,0:T(8,128)S(1)}, f32[64,128]{1,0:T(8,128)S(1)}) custom-call(s32[1]{0:T(128)} %bitcast.tile, bf16[1664,512]{1,0:T(8,128)(2,1)S(1)} %copy-done.5, s32[8,128]{1,0:T(8,128)S(1)} %get-tuple-element.25.shifts, f32[8,128]{1,0:T(8,128)S(1)} %get-tuple-element.26.info, ...), custom_call_target="tpu_custom_call" | custom-call | flops 4294967296 | bytes 1048576 | tf_op jit(solution)/shard_map/next_step/pallas_call | solution.py:686
  30.2 0.9 %collective-permute-start.11 = (f32[64,128]{1,0:T(8,128)S(1)}, f32[64,128]{1,0:T(8,128)S(1)}, u32[]{:S(2)}, u32[]{:S(2)}) collective-permute-start(f32[64,128]{1,0:T(8,128)S(1)} %get-tuple-element.37.refs_0_), channel_id=1, source_target_pairs={{0,2},{1,3},{2,0},{3,1},{4,6},{5,7},{6,4},{7,5},{8,10},{9,11},{10,... | collective-permute-start | bytes 98312 | tf_op jit(solution)/shard_map/ppermute | solution.py:556
  31.1 0.8 %collective-permute-start.12 = (f32[64,128]{1,0:T(8,128)S(1)}, f32[64,128]{1,0:T(8,128)S(1)}, u32[]{:S(2)}, u32[]{:S(2)}) collective-permute-start(f32[64,128]{1,0:T(8,128)S(1)} %get-tuple-element.37.refs_0_), channel_id=1, source_target_pairs={{0,3},{1,2},{2,1},{3,0},{4,7},{5,6},{6,5},{7,4},{8,11},{9,10},{10,... | collective-permute-start | bytes 98312 | tf_op jit(solution)/shard_map/ppermute | solution.py:556
  32.0 0.3 slope_step.1.slopes
  32.3 2.0 %collective-permute-done.11.refs_2_ = f32[64,128]{1,0:T(8,128)S(1)} collective-permute-done((f32[64,128]{1,0:T(8,128)S(1)}, f32[64,128]{1,0:T(8,128)S(1)}, u32[]{:S(2)}, u32[]{:S(2)}) %collective-permute-start.11) | collective-permute-done | bytes 32800 | tf_op jit(solution)/shard_map/ppermute | solution.py:556
  34.2 0.5 %collective-permute-done.12.refs_3_ = f32[64,128]{1,0:T(8,128)S(1)} collective-permute-done((f32[64,128]{1,0:T(8,128)S(1)}, f32[64,128]{1,0:T(8,128)S(1)}, u32[]{:S(2)}, u32[]{:S(2)}) %collective-permute-start.12) | collective-permute-done | bytes 32800 | tf_op jit(solution)/shard_map/ppermute | solution.py:556
  34.7 3.7 %last_step.1 = (f32[256,256]{1,0:T(8,128)}, f32[8,64]{1,0:T(8,128)S(1)}) custom-call(s32[1]{0:T(128)} %bitcast.tile, bf16[1664,512]{1,0:T(8,128)(2,1)S(1)} %copy-done.5, s32[8,128]{1,0:T(8,128)S(1)} %get-tuple-element.25.shifts, f32[8,128]{1,0:T(8,128)S(1)} %get-tuple-element.26.info, f32[64,32,128]{2,1,0:T(8,128)S(1)} %get-tuple-element.27.pr, ...), custom_call_target="tpu_custom_call" | custom-call | flops 4294967296 | bytes 1048576 | tf_op jit(solution)/shard_map/last_step/pallas_call | solution.py:708
  38.6 1.0 %collective-permute-start.14 = (f32[8,64]{1,0:T(8,128)S(1)}, f32[8,64]{1,0:T(8,128)S(1)}, u32[]{:S(2)}, u32[]{:S(2)}) collective-permute-start(f32[8,64]{1,0:T(8,128)S(1)} %get-tuple-element.39.refs_0_), channel_id=1, source_target_pairs={{0,2},{1,3},{2,0},{3,1},{4,6},{5,7},{6,4},{7,5},{8,10},{9,11},{10,... | collective-permute-start | bytes 6152 | tf_op jit(solution)/shard_map/ppermute | solution.py:556
  39.6 0.7 %collective-permute-start.15 = (f32[8,64]{1,0:T(8,128)S(1)}, f32[8,64]{1,0:T(8,128)S(1)}, u32[]{:S(2)}, u32[]{:S(2)}) collective-permute-start(f32[8,64]{1,0:T(8,128)S(1)} %get-tuple-element.39.refs_0_), channel_id=1, source_target_pairs={{0,3},{1,2},{2,1},{3,0},{4,7},{5,6},{6,5},{7,4},{8,11},{9,10},{10,... | collective-permute-start | bytes 6152 | tf_op jit(solution)/shard_map/ppermute | solution.py:556
  40.3 1.9 %collective-permute-done.14.refs_2_ = f32[8,64]{1,0:T(8,128)S(1)} collective-permute-done((f32[8,64]{1,0:T(8,128)S(1)}, f32[8,64]{1,0:T(8,128)S(1)}, u32[]{:S(2)}, u32[]{:S(2)}) %collective-permute-start.14) | collective-permute-done | bytes 2080 | tf_op jit(solution)/shard_map/ppermute | solution.py:556
  42.2 0.5 %collective-permute-done.15.refs_3_ = f32[8,64]{1,0:T(8,128)S(1)} collective-permute-done((f32[8,64]{1,0:T(8,128)S(1)}, f32[8,64]{1,0:T(8,128)S(1)}, u32[]{:S(2)}, u32[]{:S(2)}) %collective-permute-start.15) | collective-permute-done | bytes 2080 | tf_op jit(solution)/shard_map/ppermute | solution.py:556
  42.6 0.8 %weight_step.1 = f32[1,16]{1,0:T(1,128)} custom-call(s32[1]{0:T(128)} %bitcast.tile, s32[1]{0:T(128)} %bitcast.1.place, f32[8,128]{1,0:T(8,128)S(1)} %get-tuple-element.26.info, f32[8,64]{1,0:T(8,128)S(1)} %get-tuple-element.39.refs_0_, f32[8,64]{1,0:T(8,128)S(1)} %collective-permute-done.13.refs_1_, f32[8,64]{1,0:T(8,128)S(1)} %collective-permute-done.14.refs_2_, ...), custom_call_target="tpu_custom_call" | custom-call | tf_op jit(solution)/shard_map/weight_step/pallas_call | solution.py:723
  (30 shorter events, 1.2 us)
Async XLA Ops:
  0.6 8.4 %copy-start.5 = (bf16[1664,512]{1,0:T(8,128)(2,1)S(1)}, bf16[1664,512]{1,0:T(8,128)(2,1)}, u32[]{:S(2)}) copy-start(bf16[1664,512]{1,0:T(8,128)(2,1)} %constant.9.clone.table) | copy-start | bytes 5111812
  0.6 6.6 %copy-start = (f32[256,256]{1,0:T(8,128)S(1)}, f32[256,256]{1,0:T(8,128)}, u32[]{:S(2)}) copy-start(f32[256,256]{1,0:T(8,128)} %refs_0_.1) | copy-start | bytes 786436
  0.7 0.8 %copy-start.2 = (f32[16]{0:T(128)S(1)}, f32[16]{0:T(128)}, u32[]{:S(2)}) copy-start(f32[16]{0:T(128)} %param.8) | copy-start | bytes 196
  0.7 0.8 %copy-start.1 = (s32[16,2]{0,1:T(2,128)S(1)}, s32[16,2]{0,1:T(2,128)}, u32[]{:S(2)}) copy-start(s32[16,2]{0,1:T(2,128)} %param.9) | copy-start | bytes 388
  0.7 8.4 %copy-start.4 = (f32[2,32,32]{2,1,0:T(8,128)S(1)}, f32[2,32,32]{2,1,0:T(8,128)}, u32[]{:S(2)}) copy-start(f32[2,32,32]{2,1,0:T(8,128)} %pupil.1) | copy-start | bytes 24580
  0.7 8.4 %copy-start.3 = (f32[256,256]{1,0:T(8,128)S(1)}, f32[256,256]{1,0:T(8,128)}, u32[]{:S(2)}) copy-start(f32[256,256]{1,0:T(8,128)} %goal.1) | copy-start | bytes 786436
  0.7 8.3 %collective-permute-start = (f32[256,256]{1,0:T(8,128)}, f32[256,256]{1,0:T(8,128)S(1)}, u32[]{:S(2)}, u32[]{:S(2)}) collective-permute-start(f32[256,256]{1,0:T(8,128)} %refs_0_.1), channel_id=1, source_target_pairs={{0,1},{1,0},{2,3},{3,2},{4,5},{5,4},{6,7},{7,6},{8,9},{9,8},{10,11... | collective-permute-start | bytes 786440 | tf_op jit(solution)/shard_map/ppermute | solution.py:556
  1.6 7.9 %collective-permute-start.2 = (f32[8,128]{1,0:T(8,128)S(1)}, f32[8,128]{1,0:T(8,128)S(1)}, u32[]{:S(2)}, u32[]{:S(2)}) collective-permute-start(f32[8,128]{1,0:T(8,128)S(1)} %pack_sources.1.refs_0_), channel_id=1, source_target_pairs={{0,4},{4,0},{8,12},{12,8},{1,5},{5,1},{9,13},{13,9},{2,6},{6,2},{1... | collective-permute-start | bytes 12296 | tf_op jit(solution)/shard_map/ppermute | solution.py:556
  4.6 4.9 %collective-permute-start.3 = (f32[8,128]{1,0:T(8,128)S(1)}, f32[8,128]{1,0:T(8,128)S(1)}, u32[]{:S(2)}, u32[]{:S(2)}) collective-permute-start(f32[8,128]{1,0:T(8,128)S(1)} %pack_sources.1.refs_0_), channel_id=1, source_target_pairs={{0,8},{4,12},{8,0},{12,4},{1,9},{5,13},{9,1},{13,5},{2,10},{6,14},... | collective-permute-start | bytes 12296 | tf_op jit(solution)/shard_map/ppermute | solution.py:556
  7.2 5.4 %collective-permute-start.4 = (f32[8,128]{1,0:T(8,128)S(1)}, f32[8,128]{1,0:T(8,128)S(1)}, u32[]{:S(2)}, u32[]{:S(2)}) collective-permute-start(f32[8,128]{1,0:T(8,128)S(1)} %pack_sources.1.refs_0_), channel_id=1, source_target_pairs={{0,12},{4,8},{8,4},{12,0},{1,13},{5,9},{9,5},{13,1},{2,14},{6,10},... | collective-permute-start | bytes 12296 | tf_op jit(solution)/shard_map/ppermute | solution.py:556
  7.2 12.0 %collective-permute-start.5 = (f32[256,256]{1,0:T(8,128)S(1)}, f32[256,256]{1,0:T(8,128)S(1)}, u32[]{:S(2)}, u32[]{:S(2)}) collective-permute-start(f32[256,256]{1,0:T(8,128)S(1)} %copy-done), channel_id=1, source_target_pairs={{0,2},{1,3},{2,0},{3,1},{4,6},{5,7},{6,4},{7,5},{8,10},{9,11},{10,... | collective-permute-start | bytes 786440 | tf_op jit(solution)/shard_map/ppermute | solution.py:556
  9.0 6.2 %collective-permute-start.1 = (f32[64,256]{1,0:T(8,128)S(1)}, f32[64,256]{1,0:T(8,128)S(1)}, u32[]{:S(2)}, u32[]{:S(2)}) collective-permute-start(f32[64,256]{1,0:T(8,128)S(1)} %edge_rows.1), channel_id=1, source_target_pairs={{1,2},{3,0},{2,1},{0,3},{5,6},{7,4},{6,5},{4,7},{9,10},{11,8},{10,... | collective-permute-start | bytes 196616 | tf_op jit(solution)/shard_map/ppermute | solution.py:622
  19.2 5.8 %collective-permute-start.6 = (f32[256,256]{1,0:T(8,128)S(1)}, f32[256,256]{1,0:T(8,128)S(1)}, u32[]{:S(2)}, u32[]{:S(2)}) collective-permute-start(f32[256,256]{1,0:T(8,128)S(1)} %collective-permute-done.5.refs_0_.refs_2_), channel_id=1, source_target_pairs={{0,1},{1,0},{2,3},{3,2},{4,5},{5,4},{6,7},{7,6},{8,9},{9,8},{10,11... | collective-permute-start | bytes 786440 | tf_op jit(solution)/shard_map/ppermute | solution.py:556
  20.1 1.9 %collective-permute-start.7 = (f32[64,128]{1,0:T(8,128)S(1)}, f32[64,128]{1,0:T(8,128)S(1)}, u32[]{:S(2)}, u32[]{:S(2)}) collective-permute-start(f32[64,128]{1,0:T(8,128)S(1)} %get-tuple-element.31.value), channel_id=1, source_target_pairs={{0,1},{1,0},{2,3},{3,2},{4,5},{5,4},{6,7},{7,6},{8,9},{9,8},{10,11... | collective-permute-start | bytes 98312 | tf_op jit(solution)/shard_map/ppermute | solution.py:556
  20.2 3.9 %collective-permute-start.8 = (f32[64,128]{1,0:T(8,128)S(1)}, f32[64,128]{1,0:T(8,128)S(1)}, u32[]{:S(2)}, u32[]{:S(2)}) collective-permute-start(f32[64,128]{1,0:T(8,128)S(1)} %get-tuple-element.31.value), channel_id=1, source_target_pairs={{0,2},{1,3},{2,0},{3,1},{4,6},{5,7},{6,4},{7,5},{8,10},{9,11},{10,... | collective-permute-start | bytes 98312 | tf_op jit(solution)/shard_map/ppermute | solution.py:556
  21.7 3.4 %collective-permute-start.9 = (f32[64,128]{1,0:T(8,128)S(1)}, f32[64,128]{1,0:T(8,128)S(1)}, u32[]{:S(2)}, u32[]{:S(2)}) collective-permute-start(f32[64,128]{1,0:T(8,128)S(1)} %get-tuple-element.31.value), channel_id=1, source_target_pairs={{0,3},{1,2},{2,1},{3,0},{4,7},{5,6},{6,5},{7,4},{8,11},{9,10},{10,... | collective-permute-start | bytes 98312 | tf_op jit(solution)/shard_map/ppermute | solution.py:556
  30.0 2.2 %collective-permute-start.10 = (f32[64,128]{1,0:T(8,128)S(1)}, f32[64,128]{1,0:T(8,128)S(1)}, u32[]{:S(2)}, u32[]{:S(2)}) collective-permute-start(f32[64,128]{1,0:T(8,128)S(1)} %get-tuple-element.37.refs_0_), channel_id=1, source_target_pairs={{0,1},{1,0},{2,3},{3,2},{4,5},{5,4},{6,7},{7,6},{8,9},{9,8},{10,11... | collective-permute-start | bytes 98312 | tf_op jit(solution)/shard_map/ppermute | solution.py:556
  30.2 4.0 %collective-permute-start.11 = (f32[64,128]{1,0:T(8,128)S(1)}, f32[64,128]{1,0:T(8,128)S(1)}, u32[]{:S(2)}, u32[]{:S(2)}) collective-permute-start(f32[64,128]{1,0:T(8,128)S(1)} %get-tuple-element.37.refs_0_), channel_id=1, source_target_pairs={{0,2},{1,3},{2,0},{3,1},{4,6},{5,7},{6,4},{7,5},{8,10},{9,11},{10,... | collective-permute-start | bytes 98312 | tf_op jit(solution)/shard_map/ppermute | solution.py:556
  31.1 3.6 %collective-permute-start.12 = (f32[64,128]{1,0:T(8,128)S(1)}, f32[64,128]{1,0:T(8,128)S(1)}, u32[]{:S(2)}, u32[]{:S(2)}) collective-permute-start(f32[64,128]{1,0:T(8,128)S(1)} %get-tuple-element.37.refs_0_), channel_id=1, source_target_pairs={{0,3},{1,2},{2,1},{3,0},{4,7},{5,6},{6,5},{7,4},{8,11},{9,10},{10,... | collective-permute-start | bytes 98312 | tf_op jit(solution)/shard_map/ppermute | solution.py:556
  38.4 1.9 %collective-permute-start.13 = (f32[8,64]{1,0:T(8,128)S(1)}, f32[8,64]{1,0:T(8,128)S(1)}, u32[]{:S(2)}, u32[]{:S(2)}) collective-permute-start(f32[8,64]{1,0:T(8,128)S(1)} %get-tuple-element.39.refs_0_), channel_id=1, source_target_pairs={{0,1},{1,0},{2,3},{3,2},{4,5},{5,4},{6,7},{7,6},{8,9},{9,8},{10,11... | collective-permute-start | bytes 6152 | tf_op jit(solution)/shard_map/ppermute | solution.py:556
  38.6 3.6 %collective-permute-start.14 = (f32[8,64]{1,0:T(8,128)S(1)}, f32[8,64]{1,0:T(8,128)S(1)}, u32[]{:S(2)}, u32[]{:S(2)}) collective-permute-start(f32[8,64]{1,0:T(8,128)S(1)} %get-tuple-element.39.refs_0_), channel_id=1, source_target_pairs={{0,2},{1,3},{2,0},{3,1},{4,6},{5,7},{6,4},{7,5},{8,10},{9,11},{10,... | collective-permute-start | bytes 6152 | tf_op jit(solution)/shard_map/ppermute | solution.py:556
  39.6 3.0 %collective-permute-start.15 = (f32[8,64]{1,0:T(8,128)S(1)}, f32[8,64]{1,0:T(8,128)S(1)}, u32[]{:S(2)}, u32[]{:S(2)}) collective-permute-start(f32[8,64]{1,0:T(8,128)S(1)} %get-tuple-element.39.refs_0_), channel_id=1, source_target_pairs={{0,3},{1,2},{2,1},{3,0},{4,7},{5,6},{6,5},{7,4},{8,11},{9,10},{10,... | collective-permute-start | bytes 6152 | tf_op jit(solution)/shard_map/ppermute | solution.py:556
where the time goes:
time: 43.6 us; the launch traced here: 43.4 us
  starting transfers between devices  14.6 us (33%)
  Pallas kernels  14.3 us (33%)
  waiting for transfers between devices  13.5 us (31%)
  between operations  0.8 us (2%)
    ppermute x15, starting transfers between devices, crossed(): lax.ppermute(value, axis, [(i, i ^ k) for i in range(lax.axis_size(axis))])  14.5 us
    ppermute x15, waiting for transfers between devices, crossed(): lax.ppermute(value, axis, [(i, i ^ k) for i in range(lax.axis_size(axis))])  10.9 us
    pallas_call x1, Pallas kernels, per_device(): pl.pallas_call(functools.partial(next_kernel, spots, tiles, scale), out_s...  4.96 us
    pallas_call x1, Pallas kernels, per_device(): pl.pallas_call(functools.partial(first_kernel, spots, peers, tiles, scale...  4.06 us
    pallas_call x1, Pallas kernels, per_device(): pl.pallas_call(functools.partial(last_kernel, spots, tiles), out_shape=[s...  3.71 us
    ppermute x1, waiting for transfers between devices, per_device(): cross = lax.ppermute(edge, 'tile', pairs + [(j, i) for i, j in pairs])  2.53 us
  transfers between devices with their start and end apart: 16, of which 8 were waited for; matrix products, arithmetic and copies ran while one was open for 0% of the time, Pallas kernels for 11%

commit v1 on v0

--- a/solution.py
+++ b/solution.py
@@ -17,6 +17,7 @@
 WEIGHT_RATE = 0.3
 TINY_EPS = 1e-06
 CHUNK = 32
+FIRST_CHUNK = 16
 GROUP = 2
 
 
@@ -152,8 +153,7 @@
     return both[:grid] + lane_sign(grid, 2 * grid, 1.0) * swap(both[grid:])
 
 
-def skewed(count, stages, first, second, carry):
-    chunks = count // CHUNK
+def skewed(chunks, stages, first, second, carry):
     first(0, stages[0])
     for c in range(1, chunks):
         first(c, stages[c % 2])
@@ -190,14 +190,15 @@
     plain, crossed, fields, *stages = work
     count, grid, lanes = fields.shape
     box_len = t["row_fwd"].shape[1] // 6
+    size = stages[0].shape[0] // box_len
     plain[...] = spec
     crossed[...] = swap(spec)
     sign = lane_sign(box_len, lanes, -1.0)
 
     def first(c, stage):
         rows = []
-        for i in range(CHUNK):
-            s = c * CHUNK + i
+        for i in range(size):
+            s = c * size + i
             at = pl.ds(shifts[1, s] + MAX_SHIFT, box_len)
             real, imag = pupils(s)
             high, low = split(real * plain[at, :] + imag * crossed[at, :])
@@ -205,7 +206,7 @@
         stage[...] = halves(dot(jnp.concatenate(rows, 0), t["lane_fwd"][...]))
 
     def second(c, stage, power):
-        for base in range(0, CHUNK, GROUP):
+        for base in range(0, size, GROUP):
             stacks = []
             for i in range(base, base + GROUP):
                 part = stage[i * box_len : (i + 1) * box_len, :]
@@ -215,11 +216,11 @@
             for i in range(GROUP):
                 field = out[:, i * lanes : (i + 1) * lanes]
                 square = field * field
-                fields[c * CHUNK + base + i] = square if squares else field
+                fields[c * size + base + i] = square if squares else field
                 power = power + square
         return power
 
-    return skewed(count, stages, first, second, jnp.zeros((grid, lanes), f32))
+    return skewed(count // size, stages, first, second, jnp.zeros((grid, lanes), f32))
 
 
 def grid_misfit(power, inv_dose, target, t):
@@ -233,15 +234,16 @@
 def gather_back(misfit, shifts, scale, t, pr, pi, fields, stages, sums):
     count, box_len, lanes = pr.shape
     grid = lanes // 2
+    size = stages[0].shape[0] // box_len
     for ref in sums:
         ref[...] = jnp.zeros_like(ref)
     sign = lane_sign(box_len, lanes, 1.0)
 
     def first(c, stage):
-        for base in range(0, CHUNK, GROUP):
+        for base in range(0, size, GROUP):
             stacks = []
             for i in range(base, base + GROUP):
-                high, low = split(fields[c * CHUNK + i] * misfit)
+                high, low = split(fields[c * size + i] * misfit)
                 stacks.append(jnp.concatenate([high, low, high], 0))
             both = dot(t["row_back"][...], jnp.concatenate(stacks, 1))
             for i in range(GROUP):
@@ -252,8 +254,8 @@
     def second(c, stage, carry):
         high, low = split(stage[...])
         hits = halves(dot(jnp.concatenate([high, low], 1), t["lane_back"][...]))
-        for i in range(CHUNK):
-            s = c * CHUNK + i
+        for i in range(size):
+            s = c * size + i
             rows = pl.ds(shifts[1, s] + MAX_SHIFT, box_len)
             hit = hits[i * box_len : (i + 1) * box_len]
             one, two = sums[2 * (i % 2)], sums[2 * (i % 2) + 1]
@@ -261,7 +263,7 @@
             two[rows, :] += pi[s] * hit
         return carry
 
-    skewed(count, stages, first, second, 0)
+    skewed(count // size, stages, first, second, 0)
     whole, turned = sums[0], sums[1]
     whole[...] = (whole[...] + sums[2][...] + swap(turned[...] + sums[3][...])) * scale
     middle = grid // 2
@@ -625,13 +627,17 @@
 
     whole, spots = pack_tables(tables)
     table = jnp.asarray(whole)
-    work = [
-        pltpu.VMEM((grid, lanes), f32),
-        pltpu.VMEM((grid, lanes), f32),
-        pltpu.VMEM((count, grid, lanes), f32),
-        pltpu.VMEM((CHUNK * box_len, lanes), f32),
-        pltpu.VMEM((CHUNK * box_len, lanes), f32),
-    ]
+
+    def work_of(chunk):
+        return [
+            pltpu.VMEM((grid, lanes), f32),
+            pltpu.VMEM((grid, lanes), f32),
+            pltpu.VMEM((count, grid, lanes), f32),
+            pltpu.VMEM((chunk * box_len, lanes), f32),
+            pltpu.VMEM((chunk * box_len, lanes), f32),
+        ]
+
+    work = work_of(CHUNK)
     hold = [pltpu.VMEM((grid, lanes), f32)] * 4
     period = tile_len + 2 * MARGIN
     steps = [pltpu.VMEM((tiles + 2, period, tile_len), f32)]
@@ -656,7 +662,7 @@
                    struct(8, 128, kind=jnp.int32), struct(period, tile_len)],
         in_specs=[smem] + [vmem] * (7 + peers),
         out_specs=[vmem] * 6,
-        scratch_shapes=work + hold + [
+        scratch_shapes=work_of(FIRST_CHUNK) + hold + [
             pltpu.SMEM((8, 128), jnp.int32),
             pltpu.SMEM((8, 128), f32),
             pltpu.SemaphoreType.DMA((2,)),

time: 43.6 us -> 43.6 us (level)
  no operation moved by 1% of the time
where the time goes in v1:
time: 43.6 us; the launch traced here: 43.4 us
  starting transfers between devices  14.6 us (33%)
  Pallas kernels  14.4 us (33%)
  waiting for transfers between devices  13.4 us (31%)
  between operations  0.8 us (2%)
    ppermute x15, starting transfers between devices, crossed(): lax.ppermute(value, axis, [(i, i ^ k) for i in range(lax.axis_size(axis))])  14.5 us
    ppermute x15, waiting for transfers between devices, crossed(): lax.ppermute(value, axis, [(i, i ^ k) for i in range(lax.axis_size(axis))])  10.9 us
    pallas_call x1, Pallas kernels, per_device(): pl.pallas_call(functools.partial(next_kernel, spots, tiles, scale), out_s...  4.97 us
    pallas_call x1, Pallas kernels, per_device(): pl.pallas_call(functools.partial(first_kernel, spots, peers, tiles, scale...  4.11 us
    pallas_call x1, Pallas kernels, per_device(): pl.pallas_call(functools.partial(last_kernel, spots, tiles), out_shape=[s...  3.71 us
    ppermute x1, waiting for transfers between devices, per_device(): cross = lax.ppermute(edge, 'tile', pairs + [(j, i) for i, j in pairs])  2.53 us
  transfers between devices with their start and end apart: 16, of which 8 were waited for; matrix products, arithmetic and copies ran while one was open for 0% of the time, Pallas kernels for 11%

profile of v1, /device:TPU:0, one launch (start us, length us, event | category | flops | bytes accessed | tf_op | source)
XLA Modules:
  0.0 43.4 jit_solution(11270409685336299120)
XLA Ops:
  0.7 0.6 %collective-permute-start = (f32[256,256]{1,0:T(8,128)}, f32[256,256]{1,0:T(8,128)S(1)}, u32[]{:S(2)}, u32[]{:S(2)}) collective-permute-start(f32[256,256]{1,0:T(8,128)} %refs_0_.1), channel_id=1, source_target_pairs={{0,1},{1,0},{2,3},{3,2},{4,5},{5,4},{6,7},{7,6},{8,9},{9,8},{10,11... | collective-permute-start | bytes 786440 | tf_op jit(solution)/shard_map/ppermute | solution.py:558
  1.6 3.1 %collective-permute-start.2 = (f32[8,128]{1,0:T(8,128)S(1)}, f32[8,128]{1,0:T(8,128)S(1)}, u32[]{:S(2)}, u32[]{:S(2)}) collective-permute-start(f32[8,128]{1,0:T(8,128)S(1)} %pack_sources.1.refs_0_), channel_id=1, source_target_pairs={{0,4},{4,0},{8,12},{12,8},{1,5},{5,1},{9,13},{13,9},{2,6},{6,2},{1... | collective-permute-start | bytes 12296 | tf_op jit(solution)/shard_map/ppermute | solution.py:558
  4.6 2.6 %collective-permute-start.3 = (f32[8,128]{1,0:T(8,128)S(1)}, f32[8,128]{1,0:T(8,128)S(1)}, u32[]{:S(2)}, u32[]{:S(2)}) collective-permute-start(f32[8,128]{1,0:T(8,128)S(1)} %pack_sources.1.refs_0_), channel_id=1, source_target_pairs={{0,8},{4,12},{8,0},{12,4},{1,9},{5,13},{9,1},{13,5},{2,10},{6,14},... | collective-permute-start | bytes 12296 | tf_op jit(solution)/shard_map/ppermute | solution.py:558
  7.2 1.7 %collective-permute-start.5 = (f32[256,256]{1,0:T(8,128)S(1)}, f32[256,256]{1,0:T(8,128)S(1)}, u32[]{:S(2)}, u32[]{:S(2)}) collective-permute-start(f32[256,256]{1,0:T(8,128)S(1)} %copy-done), channel_id=1, source_target_pairs={{0,2},{1,3},{2,0},{3,1},{4,6},{5,7},{6,4},{7,5},{8,10},{9,11},{10,... | collective-permute-start | bytes 786440 | tf_op jit(solution)/shard_map/ppermute | solution.py:558
  9.1 0.4 early_step.1
  9.5 3.1 %collective-permute-done.4.refs_3_ = f32[8,128]{1,0:T(8,128)S(1)} collective-permute-done((f32[8,128]{1,0:T(8,128)S(1)}, f32[8,128]{1,0:T(8,128)S(1)}, u32[]{:S(2)}, u32[]{:S(2)}) %collective-permute-start.4) | collective-permute-done | bytes 4128 | tf_op jit(solution)/shard_map/ppermute | solution.py:558
  12.6 2.5 %collective-permute-done.1.cross = f32[64,256]{1,0:T(8,128)S(1)} collective-permute-done((f32[64,256]{1,0:T(8,128)S(1)}, f32[64,256]{1,0:T(8,128)S(1)}, u32[]{:S(2)}, u32[]{:S(2)}) %collective-permute-start.1) | collective-permute-done | bytes 65568 | tf_op jit(solution)/shard_map/ppermute | solution.py:624
  15.1 4.1 %first_step.1 = (f32[64,128]{1,0:T(8,128)S(1)}, f32[64,32,128]{2,1,0:T(8,128)S(1)}, f32[64,32,128]{2,1,0:T(8,128)S(1)}, f32[8,128]{1,0:T(8,128)S(1)}, s32[8,128]{1,0:T(8,128)S(1)}, /*index=5*/f32[384,256]{1,0:T(8,128)S(1)}) custom-call(s32[1]{0:T(128)} %bitcast.tile, bf16[1664,512]{1,0:T(8,128)(2,1)S(1)} %copy-done.5, f32[256,256]{1,0:T(8,128)S(1)} %copy-done, ...), custom_call_target="tpu_custom_call" | custom-call | flops 4294967296 | bytes 1048576 | tf_op jit(solution)/shard_map/first_step/pallas_call | solution.py:659
  19.3 0.8 %collective-permute-start.6 = (f32[256,256]{1,0:T(8,128)S(1)}, f32[256,256]{1,0:T(8,128)S(1)}, u32[]{:S(2)}, u32[]{:S(2)}) collective-permute-start(f32[256,256]{1,0:T(8,128)S(1)} %collective-permute-done.5.refs_0_.refs_2_), channel_id=1, source_target_pairs={{0,1},{1,0},{2,3},{3,2},{4,5},{5,4},{6,7},{7,6},{8,9},{9,8},{10,11... | collective-permute-start | bytes 786440 | tf_op jit(solution)/shard_map/ppermute | solution.py:558
  20.2 1.5 %collective-permute-start.8 = (f32[64,128]{1,0:T(8,128)S(1)}, f32[64,128]{1,0:T(8,128)S(1)}, u32[]{:S(2)}, u32[]{:S(2)}) collective-permute-start(f32[64,128]{1,0:T(8,128)S(1)} %get-tuple-element.31.value), channel_id=1, source_target_pairs={{0,2},{1,3},{2,0},{3,1},{4,6},{5,7},{6,4},{7,5},{8,10},{9,11},{10,... | collective-permute-start | bytes 98312 | tf_op jit(solution)/shard_map/ppermute | solution.py:558
  22.0 2.1 %collective-permute-done.8.refs_4_ = f32[64,128]{1,0:T(8,128)S(1)} collective-permute-done((f32[64,128]{1,0:T(8,128)S(1)}, f32[64,128]{1,0:T(8,128)S(1)}, u32[]{:S(2)}, u32[]{:S(2)}) %collective-permute-start.8) | collective-permute-done | bytes 32800 | tf_op jit(solution)/shard_map/ppermute | solution.py:558
  24.1 1.0 %collective-permute-done.9.refs_5_ = f32[64,128]{1,0:T(8,128)S(1)} collective-permute-done((f32[64,128]{1,0:T(8,128)S(1)}, f32[64,128]{1,0:T(8,128)S(1)}, u32[]{:S(2)}, u32[]{:S(2)}) %collective-permute-start.9) | collective-permute-done | bytes 32800 | tf_op jit(solution)/shard_map/ppermute | solution.py:558
  25.1 5.0 %next_step.1 = (f32[384,256]{1,0:T(8,128)S(1)}, f32[4,256,256]{2,1,0:T(8,128)S(1)}, f32[8,128]{1,0:T(8,128)S(1)}, f32[64,128]{1,0:T(8,128)S(1)}) custom-call(s32[1]{0:T(128)} %bitcast.tile, bf16[1664,512]{1,0:T(8,128)(2,1)S(1)} %copy-done.5, s32[8,128]{1,0:T(8,128)S(1)} %get-tuple-element.25.shifts, f32[8,128]{1,0:T(8,128)S(1)} %get-tuple-element.26.info, ...), custom_call_target="tpu_custom_call" | custom-call | flops 4294967296 | bytes 1048576 | tf_op jit(solution)/shard_map/next_step/pallas_call | solution.py:692
  30.3 0.9 %collective-permute-start.11 = (f32[64,128]{1,0:T(8,128)S(1)}, f32[64,128]{1,0:T(8,128)S(1)}, u32[]{:S(2)}, u32[]{:S(2)}) collective-permute-start(f32[64,128]{1,0:T(8,128)S(1)} %get-tuple-element.37.refs_0_), channel_id=1, source_target_pairs={{0,2},{1,3},{2,0},{3,1},{4,6},{5,7},{6,4},{7,5},{8,10},{9,11},{10,... | collective-permute-start | bytes 98312 | tf_op jit(solution)/shard_map/ppermute | solution.py:558
  31.1 0.9 %collective-permute-start.12 = (f32[64,128]{1,0:T(8,128)S(1)}, f32[64,128]{1,0:T(8,128)S(1)}, u32[]{:S(2)}, u32[]{:S(2)}) collective-permute-start(f32[64,128]{1,0:T(8,128)S(1)} %get-tuple-element.37.refs_0_), channel_id=1, source_target_pairs={{0,3},{1,2},{2,1},{3,0},{4,7},{5,6},{6,5},{7,4},{8,11},{9,10},{10,... | collective-permute-start | bytes 98312 | tf_op jit(solution)/shard_map/ppermute | solution.py:558
  32.0 0.3 slope_step.1.slopes
  32.3 2.0 %collective-permute-done.11.refs_2_ = f32[64,128]{1,0:T(8,128)S(1)} collective-permute-done((f32[64,128]{1,0:T(8,128)S(1)}, f32[64,128]{1,0:T(8,128)S(1)}, u32[]{:S(2)}, u32[]{:S(2)}) %collective-permute-start.11) | collective-permute-done | bytes 32800 | tf_op jit(solution)/shard_map/ppermute | solution.py:558
  34.3 0.5 %collective-permute-done.12.refs_3_ = f32[64,128]{1,0:T(8,128)S(1)} collective-permute-done((f32[64,128]{1,0:T(8,128)S(1)}, f32[64,128]{1,0:T(8,128)S(1)}, u32[]{:S(2)}, u32[]{:S(2)}) %collective-permute-start.12) | collective-permute-done | bytes 32800 | tf_op jit(solution)/shard_map/ppermute | solution.py:558
  34.7 3.7 %last_step.1 = (f32[256,256]{1,0:T(8,128)}, f32[8,64]{1,0:T(8,128)S(1)}) custom-call(s32[1]{0:T(128)} %bitcast.tile, bf16[1664,512]{1,0:T(8,128)(2,1)S(1)} %copy-done.5, s32[8,128]{1,0:T(8,128)S(1)} %get-tuple-element.25.shifts, f32[8,128]{1,0:T(8,128)S(1)} %get-tuple-element.26.info, f32[64,32,128]{2,1,0:T(8,128)S(1)} %get-tuple-element.27.pr, ...), custom_call_target="tpu_custom_call" | custom-call | flops 4294967296 | bytes 1048576 | tf_op jit(solution)/shard_map/last_step/pallas_call | solution.py:714
  38.6 1.0 %collective-permute-start.14 = (f32[8,64]{1,0:T(8,128)S(1)}, f32[8,64]{1,0:T(8,128)S(1)}, u32[]{:S(2)}, u32[]{:S(2)}) collective-permute-start(f32[8,64]{1,0:T(8,128)S(1)} %get-tuple-element.39.refs_0_), channel_id=1, source_target_pairs={{0,2},{1,3},{2,0},{3,1},{4,6},{5,7},{6,4},{7,5},{8,10},{9,11},{10,... | collective-permute-start | bytes 6152 | tf_op jit(solution)/shard_map/ppermute | solution.py:558
  39.6 0.7 %collective-permute-start.15 = (f32[8,64]{1,0:T(8,128)S(1)}, f32[8,64]{1,0:T(8,128)S(1)}, u32[]{:S(2)}, u32[]{:S(2)}) collective-permute-start(f32[8,64]{1,0:T(8,128)S(1)} %get-tuple-element.39.refs_0_), channel_id=1, source_target_pairs={{0,3},{1,2},{2,1},{3,0},{4,7},{5,6},{6,5},{7,4},{8,11},{9,10},{10,... | collective-permute-start | bytes 6152 | tf_op jit(solution)/shard_map/ppermute | solution.py:558
  40.4 1.9 %collective-permute-done.14.refs_2_ = f32[8,64]{1,0:T(8,128)S(1)} collective-permute-done((f32[8,64]{1,0:T(8,128)S(1)}, f32[8,64]{1,0:T(8,128)S(1)}, u32[]{:S(2)}, u32[]{:S(2)}) %collective-permute-start.14) | collective-permute-done | bytes 2080 | tf_op jit(solution)/shard_map/ppermute | solution.py:558
  42.2 0.4 %collective-permute-done.15.refs_3_ = f32[8,64]{1,0:T(8,128)S(1)} collective-permute-done((f32[8,64]{1,0:T(8,128)S(1)}, f32[8,64]{1,0:T(8,128)S(1)}, u32[]{:S(2)}, u32[]{:S(2)}) %collective-permute-start.15) | collective-permute-done | bytes 2080 | tf_op jit(solution)/shard_map/ppermute | solution.py:558
  42.7 0.8 %weight_step.1 = f32[1,16]{1,0:T(1,128)} custom-call(s32[1]{0:T(128)} %bitcast.tile, s32[1]{0:T(128)} %bitcast.1.place, f32[8,128]{1,0:T(8,128)S(1)} %get-tuple-element.26.info, f32[8,64]{1,0:T(8,128)S(1)} %get-tuple-element.39.refs_0_, f32[8,64]{1,0:T(8,128)S(1)} %collective-permute-done.13.refs_1_, f32[8,64]{1,0:T(8,128)S(1)} %collective-permute-done.14.refs_2_, ...), custom_call_target="tpu_custom_call" | custom-call | tf_op jit(solution)/shard_map/weight_step/pallas_call | solution.py:729
  (30 shorter events, 1.2 us)
Async XLA Ops:
  0.6 8.4 %copy-start.5 = (bf16[1664,512]{1,0:T(8,128)(2,1)S(1)}, bf16[1664,512]{1,0:T(8,128)(2,1)}, u32[]{:S(2)}) copy-start(bf16[1664,512]{1,0:T(8,128)(2,1)} %constant.9.clone.table) | copy-start | bytes 5111812
  0.6 6.6 %copy-start = (f32[256,256]{1,0:T(8,128)S(1)}, f32[256,256]{1,0:T(8,128)}, u32[]{:S(2)}) copy-start(f32[256,256]{1,0:T(8,128)} %refs_0_.1) | copy-start | bytes 786436
  0.7 0.8 %copy-start.2 = (f32[16]{0:T(128)S(1)}, f32[16]{0:T(128)}, u32[]{:S(2)}) copy-start(f32[16]{0:T(128)} %param.8) | copy-start | bytes 196
  0.7 0.8 %copy-start.1 = (s32[16,2]{0,1:T(2,128)S(1)}, s32[16,2]{0,1:T(2,128)}, u32[]{:S(2)}) copy-start(s32[16,2]{0,1:T(2,128)} %param.9) | copy-start | bytes 388
  0.7 8.4 %copy-start.4 = (f32[2,32,32]{2,1,0:T(8,128)S(1)}, f32[2,32,32]{2,1,0:T(8,128)}, u32[]{:S(2)}) copy-start(f32[2,32,32]{2,1,0:T(8,128)} %pupil.1) | copy-start | bytes 24580
  0.7 8.4 %copy-start.3 = (f32[256,256]{1,0:T(8,128)S(1)}, f32[256,256]{1,0:T(8,128)}, u32[]{:S(2)}) copy-start(f32[256,256]{1,0:T(8,128)} %goal.1) | copy-start | bytes 786436
  0.7 8.3 %collective-permute-start = (f32[256,256]{1,0:T(8,128)}, f32[256,256]{1,0:T(8,128)S(1)}, u32[]{:S(2)}, u32[]{:S(2)}) collective-permute-start(f32[256,256]{1,0:T(8,128)} %refs_0_.1), channel_id=1, source_target_pairs={{0,1},{1,0},{2,3},{3,2},{4,5},{5,4},{6,7},{7,6},{8,9},{9,8},{10,11... | collective-permute-start | bytes 786440 | tf_op jit(solution)/shard_map/ppermute | solution.py:558
  1.6 7.9 %collective-permute-start.2 = (f32[8,128]{1,0:T(8,128)S(1)}, f32[8,128]{1,0:T(8,128)S(1)}, u32[]{:S(2)}, u32[]{:S(2)}) collective-permute-start(f32[8,128]{1,0:T(8,128)S(1)} %pack_sources.1.refs_0_), channel_id=1, source_target_pairs={{0,4},{4,0},{8,12},{12,8},{1,5},{5,1},{9,13},{13,9},{2,6},{6,2},{1... | collective-permute-start | bytes 12296 | tf_op jit(solution)/shard_map/ppermute | solution.py:558
  4.6 4.9 %collective-permute-start.3 = (f32[8,128]{1,0:T(8,128)S(1)}, f32[8,128]{1,0:T(8,128)S(1)}, u32[]{:S(2)}, u32[]{:S(2)}) collective-permute-start(f32[8,128]{1,0:T(8,128)S(1)} %pack_sources.1.refs_0_), channel_id=1, source_target_pairs={{0,8},{4,12},{8,0},{12,4},{1,9},{5,13},{9,1},{13,5},{2,10},{6,14},... | collective-permute-start | bytes 12296 | tf_op jit(solution)/shard_map/ppermute | solution.py:558
  7.2 5.4 %collective-permute-start.4 = (f32[8,128]{1,0:T(8,128)S(1)}, f32[8,128]{1,0:T(8,128)S(1)}, u32[]{:S(2)}, u32[]{:S(2)}) collective-permute-start(f32[8,128]{1,0:T(8,128)S(1)} %pack_sources.1.refs_0_), channel_id=1, source_target_pairs={{0,12},{4,8},{8,4},{12,0},{1,13},{5,9},{9,5},{13,1},{2,14},{6,10},... | collective-permute-start | bytes 12296 | tf_op jit(solution)/shard_map/ppermute | solution.py:558
  7.2 12.1 %collective-permute-start.5 = (f32[256,256]{1,0:T(8,128)S(1)}, f32[256,256]{1,0:T(8,128)S(1)}, u32[]{:S(2)}, u32[]{:S(2)}) collective-permute-start(f32[256,256]{1,0:T(8,128)S(1)} %copy-done), channel_id=1, source_target_pairs={{0,2},{1,3},{2,0},{3,1},{4,6},{5,7},{6,4},{7,5},{8,10},{9,11},{10,... | collective-permute-start | bytes 786440 | tf_op jit(solution)/shard_map/ppermute | solution.py:558
  9.0 6.2 %collective-permute-start.1 = (f32[64,256]{1,0:T(8,128)S(1)}, f32[64,256]{1,0:T(8,128)S(1)}, u32[]{:S(2)}, u32[]{:S(2)}) collective-permute-start(f32[64,256]{1,0:T(8,128)S(1)} %edge_rows.1), channel_id=1, source_target_pairs={{1,2},{3,0},{2,1},{0,3},{5,6},{7,4},{6,5},{4,7},{9,10},{11,8},{10,... | collective-permute-start | bytes 196616 | tf_op jit(solution)/shard_map/ppermute | solution.py:624
  19.3 5.8 %collective-permute-start.6 = (f32[256,256]{1,0:T(8,128)S(1)}, f32[256,256]{1,0:T(8,128)S(1)}, u32[]{:S(2)}, u32[]{:S(2)}) collective-permute-start(f32[256,256]{1,0:T(8,128)S(1)} %collective-permute-done.5.refs_0_.refs_2_), channel_id=1, source_target_pairs={{0,1},{1,0},{2,3},{3,2},{4,5},{5,4},{6,7},{7,6},{8,9},{9,8},{10,11... | collective-permute-start | bytes 786440 | tf_op jit(solution)/shard_map/ppermute | solution.py:558
  20.1 1.9 %collective-permute-start.7 = (f32[64,128]{1,0:T(8,128)S(1)}, f32[64,128]{1,0:T(8,128)S(1)}, u32[]{:S(2)}, u32[]{:S(2)}) collective-permute-start(f32[64,128]{1,0:T(8,128)S(1)} %get-tuple-element.31.value), channel_id=1, source_target_pairs={{0,1},{1,0},{2,3},{3,2},{4,5},{5,4},{6,7},{7,6},{8,9},{9,8},{10,11... | collective-permute-start | bytes 98312 | tf_op jit(solution)/shard_map/ppermute | solution.py:558
  20.2 3.9 %collective-permute-start.8 = (f32[64,128]{1,0:T(8,128)S(1)}, f32[64,128]{1,0:T(8,128)S(1)}, u32[]{:S(2)}, u32[]{:S(2)}) collective-permute-start(f32[64,128]{1,0:T(8,128)S(1)} %get-tuple-element.31.value), channel_id=1, source_target_pairs={{0,2},{1,3},{2,0},{3,1},{4,6},{5,7},{6,4},{7,5},{8,10},{9,11},{10,... | collective-permute-start | bytes 98312 | tf_op jit(solution)/shard_map/ppermute | solution.py:558
  21.7 3.4 %collective-permute-start.9 = (f32[64,128]{1,0:T(8,128)S(1)}, f32[64,128]{1,0:T(8,128)S(1)}, u32[]{:S(2)}, u32[]{:S(2)}) collective-permute-start(f32[64,128]{1,0:T(8,128)S(1)} %get-tuple-element.31.value), channel_id=1, source_target_pairs={{0,3},{1,2},{2,1},{3,0},{4,7},{5,6},{6,5},{7,4},{8,11},{9,10},{10,... | collective-permute-start | bytes 98312 | tf_op jit(solution)/shard_map/ppermute | solution.py:558
  30.1 2.2 %collective-permute-start.10 = (f32[64,128]{1,0:T(8,128)S(1)}, f32[64,128]{1,0:T(8,128)S(1)}, u32[]{:S(2)}, u32[]{:S(2)}) collective-permute-start(f32[64,128]{1,0:T(8,128)S(1)} %get-tuple-element.37.refs_0_), channel_id=1, source_target_pairs={{0,1},{1,0},{2,3},{3,2},{4,5},{5,4},{6,7},{7,6},{8,9},{9,8},{10,11... | collective-permute-start | bytes 98312 | tf_op jit(solution)/shard_map/ppermute | solution.py:558
  30.3 4.0 %collective-permute-start.11 = (f32[64,128]{1,0:T(8,128)S(1)}, f32[64,128]{1,0:T(8,128)S(1)}, u32[]{:S(2)}, u32[]{:S(2)}) collective-permute-start(f32[64,128]{1,0:T(8,128)S(1)} %get-tuple-element.37.refs_0_), channel_id=1, source_target_pairs={{0,2},{1,3},{2,0},{3,1},{4,6},{5,7},{6,4},{7,5},{8,10},{9,11},{10,... | collective-permute-start | bytes 98312 | tf_op jit(solution)/shard_map/ppermute | solution.py:558
  31.1 3.6 %collective-permute-start.12 = (f32[64,128]{1,0:T(8,128)S(1)}, f32[64,128]{1,0:T(8,128)S(1)}, u32[]{:S(2)}, u32[]{:S(2)}) collective-permute-start(f32[64,128]{1,0:T(8,128)S(1)} %get-tuple-element.37.refs_0_), channel_id=1, source_target_pairs={{0,3},{1,2},{2,1},{3,0},{4,7},{5,6},{6,5},{7,4},{8,11},{9,10},{10,... | collective-permute-start | bytes 98312 | tf_op jit(solution)/shard_map/ppermute | solution.py:558
  38.4 1.9 %collective-permute-start.13 = (f32[8,64]{1,0:T(8,128)S(1)}, f32[8,64]{1,0:T(8,128)S(1)}, u32[]{:S(2)}, u32[]{:S(2)}) collective-permute-start(f32[8,64]{1,0:T(8,128)S(1)} %get-tuple-element.39.refs_0_), channel_id=1, source_target_pairs={{0,1},{1,0},{2,3},{3,2},{4,5},{5,4},{6,7},{7,6},{8,9},{9,8},{10,11... | collective-permute-start | bytes 6152 | tf_op jit(solution)/shard_map/ppermute | solution.py:558
  38.6 3.6 %collective-permute-start.14 = (f32[8,64]{1,0:T(8,128)S(1)}, f32[8,64]{1,0:T(8,128)S(1)}, u32[]{:S(2)}, u32[]{:S(2)}) collective-permute-start(f32[8,64]{1,0:T(8,128)S(1)} %get-tuple-element.39.refs_0_), channel_id=1, source_target_pairs={{0,2},{1,3},{2,0},{3,1},{4,6},{5,7},{6,4},{7,5},{8,10},{9,11},{10,... | collective-permute-start | bytes 6152 | tf_op jit(solution)/shard_map/ppermute | solution.py:558
  39.6 3.0 %collective-permute-start.15 = (f32[8,64]{1,0:T(8,128)S(1)}, f32[8,64]{1,0:T(8,128)S(1)}, u32[]{:S(2)}, u32[]{:S(2)}) collective-permute-start(f32[8,64]{1,0:T(8,128)S(1)} %get-tuple-element.39.refs_0_), channel_id=1, source_target_pairs={{0,3},{1,2},{2,1},{3,0},{4,7},{5,6},{6,5},{7,4},{8,11},{9,10},{10,... | collective-permute-start | bytes 6152 | tf_op jit(solution)/shard_map/ppermute | solution.py:558
